TPU v7x, 128 devices: a whole 4x4x4 slice. The times are simulated.
128 devices in a mesh: op: 16 (over x, y), sec: 8 (over z, core).
Axes of the slice: x: 4, y: 4, z: 4, core: 2. Of those that a mesh axis runs over, the one named last changes fastest.
Arguments:
- wave: bfloat16 [32, 256, 4, 256], P('op'), may hold values from -6 to 6
- sector_dims: int32 [32], replicated, may hold values from 64 to 256, as said below
- left_ops: bfloat16 [32, 128, 256, 256], P(None, ('op', 'sec')), may hold values from -0.375 to 0.375
- right_ops: bfloat16 [32, 16, 8, 256, 256], P('op', None, 'sec'), may hold values from -0.375 to 0.375
- site_ops: float32 [128, 4, 4], replicated, may hold values from -0.25 to 0.25
Outputs:
- sigma: bfloat16 [32, 256, 4, 256], P('op', 'sec')
Inputs may be any that keep to these rules, and one draw needn't show every extreme that they name: `sector_dims`: every entry is a multiple of 64, and at least one sector has exactly 256 states.
All inputs are finite; a program needn't handle non-finite values.
Results may differ from a plain program's by a relative error of at most 0.005.
Values may be sent and summed in bfloat16 or wider, within the bound.
No kernel may reach another device: no remote copies, remote signals or barrier semaphores. Data moves between devices by JAX's collectives and lax.ppermute only.
A program may use at most 128 MiB of HBM per device.

v0:
```python
import jax
import jax.numpy as jnp
from jax import lax
from jax.sharding import PartitionSpec as P


def sector_mask(sizes, width):
    places = lax.broadcasted_iota(jnp.int32, (sizes.shape[0], width), 1)
    return (places < sizes[:, None]).astype(jnp.float32)


def left_step(blocks, waves, site_mats):

    def one_sector(inputs):
        ops_block, wave_block = inputs
        first = jnp.einsum(
            "klm,mpr->klpr", ops_block, wave_block, preferred_element_type=jnp.float32
        )
        second = jnp.einsum("klpr,kqp->klqr", first, site_mats, precision=lax.Precision.HIGHEST)
        return second.astype(jnp.bfloat16)

    return lax.map(one_sector, (blocks, waves))


def shards(wave, sector_dims, left_ops, right_ops, site_ops):
    sec_count = lax.axis_size("sec")
    op_index = lax.axis_index("op")
    sec_index = lax.axis_index("sec")
    local_sectors = wave.shape[0]
    width = wave.shape[1]
    term_count = left_ops.shape[1]
    own_sizes = lax.dynamic_slice_in_dim(sector_dims, op_index * local_sectors, local_sectors)
    own_mask = sector_mask(own_sizes, width)
    masked = (
        wave.astype(jnp.float32) * own_mask[:, :, None, None] * own_mask[:, None, None, :]
    ).astype(jnp.bfloat16)
    first_term = (op_index * sec_count + sec_index) * term_count
    site_local = lax.dynamic_slice_in_dim(site_ops, first_term, term_count)
    inter = left_step(left_ops, lax.all_gather(masked, "op", axis=0, tiled=True), site_local)
    inter = lax.all_to_all(inter, "op", split_axis=0, concat_axis=1, tiled=True)
    right_local = right_ops.reshape(local_sectors, -1, width, width)
    partial_sum = jnp.einsum(
        "sklqm,skrm->slqr", inter, right_local, preferred_element_type=jnp.float32
    )
    row_count = width // sec_count
    summed = lax.psum(partial_sum, "sec")
    share = lax.dynamic_slice_in_dim(summed, sec_index * row_count, row_count, 1)
    row_mask = lax.dynamic_slice_in_dim(own_mask, sec_index * row_count, row_count, 1)
    return (share * row_mask[:, :, None, None] * own_mask[:, None, None, :]).astype(jnp.bfloat16)


def solution(mesh):
    placed = (
        P("op", None, None, None),
        P(),
        P(None, ("op", "sec"), None, None),
        P("op", None, "sec", None, None),
        P(),
    )
    return jax.shard_map(
        shards, mesh=mesh, in_specs=placed, out_specs=P("op", "sec", None, None), check_vma=False
    )
```

profile of v0, /device:TPU:0, one launch (start us, length us, event | category | flops | bytes accessed | tf_op | source)
XLA Modules:
  0.0 555.1 jit_solution(4734230497809991994)
XLA Ops:
  7.4 2.5 multiply_convert_fusion
  10.2 113.6 %all-gather.2.cloned.1.call-done = bf16[32,256,4,256]{3,1,2,0:T(8,128)(2,1)} async-done(((bf16[2,256,4,256]{3,1,2,0:T(8,128)(2,1)}), bf16[32,256,4,256]{3,1,2,0:T(8,128)(2,1)}) %all-gather.2.cloned.1.call-update) | async-done | bytes 16777232 | tf_op jit(solution)/shard_map/all_gather | solution.py:39
  123.7 153.4 %while.10 = (s32[]{:T(128)}, bf16[32,1,256,4,256]{4,2,3,1,0:T(8,128)(2,1)}, bf16[32,1,256,256]{3,2,1,0:T(8,128)(2,1)}, bf16[32,256,4,256]{3,1,2,0:T(8,128)(2,1)}, f32[1,4,4]{2,1,0:T(4,128)S(1)}, /*index=5*/s32[]{:T(128)}) while((s32[]{:T(128)}, bf16[32,1,256,4,256]{4,2,3,1,0:T(8,128)(2,1)}, bf16[32,1,256,256]{3,2,1,0:T(8,128)(2,1)}, ...), condition=%wide.region_1.2_spmd, body=%wide.region_0.1_spmd.sunk | while | flops 147062784 | bytes 4327045 | solution.py:22
  125.1 2.5 fusion.24
  129.9 2.5 fusion.24
  134.7 2.5 fusion.24
  149.1 2.5 fusion.24
  153.9 2.5 fusion.24
  158.6 2.5 fusion.24
  163.4 2.5 fusion.24
  168.2 2.5 fusion.24
  173.0 2.5 fusion.24
  177.8 2.5 fusion.24
  182.6 2.5 fusion.24
  187.4 2.5 fusion.24
  192.2 2.5 fusion.24
  196.9 2.5 fusion.24
  201.8 2.5 fusion.24
  206.6 2.5 fusion.24
  211.4 2.5 fusion.24
  221.0 2.5 fusion.24
  225.8 2.5 fusion.24
  230.6 2.5 fusion.24
  235.3 2.5 fusion.24
  240.1 2.5 fusion.24
  245.0 2.5 fusion.24
  254.5 2.5 fusion.24
  259.3 2.5 fusion.24
  273.7 2.5 fusion.24
  277.1 191.8 %all_to_all.18 = bf16[32,1,256,4,256]{4,2,3,1,0:T(8,128)(2,1)} all-to-all(bf16[32,1,256,4,256]{4,2,3,1,0:T(8,128)(2,1)} %get-tuple-element.32), channel_id=1, replica_groups=mesh['op'=16,'sec'=8] {'op'}, dimensions={0} | all-to-all | bytes 33554432 | tf_op jit(solution)/shard_map/all_to_all | solution.py:40
  468.9 9.4 %fusion.9 = f32[2,256,4,256,1]{3,1,2,0,4:T(8,128)S(1)} fusion(bf16[2,16,256,4,256]{4,2,3,0,1:T(8,128)(2,1)} %bitcast.43, bf16[2,16,1,256,256]{4,3,2,1,0:T(8,128)(2,1)} %param.10), kind=kOutput, calls=%fused_computation.11 | convolution fusion | flops 4294967296 | bytes 23068672 | tf_op jit(solution)/shard_map/sklqm,skrm->slqr/dot_general | solution.py:42
  479.9 66.6 %all-reduce.2.cloned.1.call-done = f32[2,256,4,256]{3,1,0,2:T(8,128)} async-done(((f32[2,256,4,256]{3,1,0,2:T(8,128)}), f32[2,256,4,256]{3,1,0,2:T(8,128)}) %all-reduce.2.cloned.1.call-update) | async-done | bytes 2097168 | tf_op jit(solution)/shard_map/psum | solution.py:46
  (87 shorter events, 92.8 us)
Async XLA Ops:
  6.5 3.4 copy-start
  6.5 117.2 %all-gather.2.cloned.1.call-start = ((), (), s32[]{:S(2)}) async-start(), calls=%async_computation.1 | async-start | bytes 17825792 | tf_op jit(solution)/shard_map/all_gather | solution.py:39
  9.9 536.6 %all-reduce.2.cloned.1.call-start = ((), (), s32[]{:S(2)}) async-start(), calls=%async_computation.2 | async-start | bytes 4194304 | tf_op jit(solution)/shard_map/psum | solution.py:46
  468.9 79.4 %copy-start.1 = (f32[128,4,4]{0,2,1:T(4,128)S(1)}, f32[128,4,4]{0,2,1:T(4,128)}, u32[]{:S(2)}) copy-start(f32[128,4,4]{0,2,1:T(4,128)} %param.11) | copy-start | bytes 24580
Sparse Core Ops, SparseCore 0:
  10.0 113.6 all-gather.1
  480.0 66.4 all-reduce.1
where the time goes:
time: 556 us; the launch traced here: 555 us
  blocking collectives  192 us (35%)
  waiting for transfers between devices  180 us (32%)
  matrix products  134 us (24%)
  local copies, waits for them, and re-layouts  31.5 us (6%)
  between operations  13.4 us (2%)
    all_to_all x1, blocking collectives, shards(): inter = lax.all_to_all(inter, 'op', split_axis=0, concat_axis=1, tiled=True)  192 us
    all_gather x1, waiting for transfers between devices, shards(): lax.all_gather(masked, 'op', axis=0, tiled=True)  114 us
    dot_general x32, matrix products, one_sector(): jnp.einsum('klpr,kqp->klqr', first, site_mats, precision=lax.Precision.HI...  79.6 us
    psum x1, waiting for transfers between devices, shards(): summed = lax.psum(partial_sum, 'sec')  66.6 us
    dot_general x32, matrix products, one_sector(): jnp.einsum('klm,mpr->klpr', ops_block, wave_block, preferred_element_type...  45.2 us
    dynamic_update_slice x32, local copies, waits for them, and re-layouts, left_step(): return lax.map(one_sector, (blocks, waves))  28.2 us
  transfers between devices with their start and end apart: 2, of which 2 were waited for; matrix products, arithmetic and copies ran while one was open for 0% of the time, Pallas kernels for 0%

commit v1 on v0

--- a/solution.py
+++ b/solution.py
@@ -2,6 +2,12 @@
 import jax.numpy as jnp
 from jax import lax
 from jax.sharding import PartitionSpec as P
+
+
+def gather_by_exchange(x, axis, dim):
+    count = lax.axis_size(axis)
+    repeats = [count if d == dim else 1 for d in range(x.ndim)]
+    return lax.all_to_all(jnp.tile(x, repeats), axis, split_axis=dim, concat_axis=dim, tiled=True)
 
 
 def sector_mask(sizes, width):
@@ -36,7 +42,7 @@
     ).astype(jnp.bfloat16)
     first_term = (op_index * sec_count + sec_index) * term_count
     site_local = lax.dynamic_slice_in_dim(site_ops, first_term, term_count)
-    inter = left_step(left_ops, lax.all_gather(masked, "op", axis=0, tiled=True), site_local)
+    inter = left_step(left_ops, gather_by_exchange(masked, "op", 0), site_local)
     inter = lax.all_to_all(inter, "op", split_axis=0, concat_axis=1, tiled=True)
     right_local = right_ops.reshape(local_sectors, -1, width, width)
     partial_sum = jnp.einsum(

time: 556 us -> 792 us (1.42)
  waiting for transfers between devices: 180 us -> 363 us
  local copies, waits for them, and re-layouts: 31.5 us -> 76.9 us
    all_to_all x0 -> x1, waiting for transfers between devices: none -> 293 us  [gather_by_exchange(): lax.all_to_all(jnp.tile(x, repeats), axis, split_axis=dim, concat_axis=di...]
    all_gather x1 -> x0, waiting for transfers between devices: 114 us -> none  [shards(): lax.all_gather(masked, 'op', axis=0, tiled=True)]
    squeeze x0 -> x32, local copies, waits for them, and re-layouts: none -> 39.1 us  [left_step(): return lax.map(one_sector, (blocks, waves))]
where the time goes in v1:
time: 792 us; the launch traced here: 790 us
  waiting for transfers between devices  363 us (46%)
  blocking collectives  198 us (25%)
  matrix products  128 us (16%)
  local copies, waits for them, and re-layouts  76.9 us (10%)
  between operations  13.5 us (2%)
    all_to_all x1, waiting for transfers between devices, gather_by_exchange(): lax.all_to_all(jnp.tile(x, repeats), axis, split_axis=dim, concat_axis=di...  293 us
    all_to_all x1, blocking collectives, shards(): inter = lax.all_to_all(inter, 'op', split_axis=0, concat_axis=1, tiled=True)  198 us
    dot_general x32, matrix products, one_sector(): jnp.einsum('klpr,kqp->klqr', first, site_mats, precision=lax.Precision.HI...  79.6 us
    psum x1, waiting for transfers between devices, shards(): summed = lax.psum(partial_sum, 'sec')  70.5 us
    squeeze x32, local copies, waits for them, and re-layouts, left_step(): return lax.map(one_sector, (blocks, waves))  39.1 us
    dot_general x32, matrix products, one_sector(): jnp.einsum('klm,mpr->klpr', ops_block, wave_block, preferred_element_type...  38.7 us
    dynamic_update_slice x32, local copies, waits for them, and re-layouts, left_step(): return lax.map(one_sector, (blocks, waves))  28.2 us
  transfers between devices with their start and end apart: 2, of which 2 were waited for; matrix products, arithmetic and copies ran while one was open for 0% of the time, Pallas kernels for 0%

profile of v1, /device:TPU:0, one launch (start us, length us, event | category | flops | bytes accessed | tf_op | source)
XLA Modules:
  0.0 789.7 jit_solution(14845069868140764267)
XLA Ops:
  9.1 7.8 tile.4
  16.9 7.2 all-to-all-start
  24.4 292.8 %all-to-all-done = bf16[32,256,4,256]{3,2,1,0:T(4,128)(2,1)} async-done(((bf16[32,256,4,256]{3,2,1,0:T(4,128)(2,1)}), bf16[32,256,4,256]{3,2,1,0:T(4,128)(2,1)}, u32[]{:S(2)}, u32[]{:S(2)}) %all-to-all-start) | async-done | bytes 16777248 | tf_op jit(solution)/shard_map/all_to_all | solution.py:10
  317.2 186.0 %while.10 = (s32[]{:T(128)}, bf16[32,1,256,4,256]{4,2,3,1,0:T(8,128)(2,1)}, bf16[32,1,256,256]{3,2,1,0:T(8,128)(2,1)}, bf16[32,256,4,256]{3,2,1,0:T(4,128)(2,1)}, f32[1,4,4]{2,1,0:T(4,128)S(1)}, /*index=5*/s32[]{:T(128)}) while((s32[]{:T(128)}, bf16[32,1,256,4,256]{4,2,3,1,0:T(8,128)(2,1)}, bf16[32,1,256,256]{3,2,1,0:T(8,128)(2,1)}, ...), condition=%wide.region_1.2_spmd, body=%wide.region_0.1_spmd.sunk | while | flops 147062784 | bytes 5375113 | solution.py:28
  319.6 2.5 fusion.28
  325.4 2.5 fusion.28
  331.2 2.5 fusion.28
  337.1 2.5 fusion.28
  342.9 2.5 fusion.28
  348.7 2.5 fusion.28
  354.5 2.5 fusion.28
  360.3 2.5 fusion.28
  366.1 2.5 fusion.28
  371.9 2.5 fusion.28
  377.7 2.5 fusion.28
  383.5 2.5 fusion.28
  389.4 2.5 fusion.28
  395.2 2.5 fusion.28
  401.0 2.5 fusion.28
  406.8 2.5 fusion.28
  418.5 2.5 fusion.28
  424.3 2.5 fusion.28
  430.1 2.5 fusion.28
  435.9 2.5 fusion.28
  441.8 2.5 fusion.28
  447.5 2.5 fusion.28
  453.3 2.5 fusion.28
  459.2 2.5 fusion.28
  470.8 2.5 fusion.28
  503.2 197.7 %all_to_all.23 = bf16[32,1,256,4,256]{4,2,3,1,0:T(8,128)(2,1)} all-to-all(bf16[32,1,256,4,256]{4,2,3,1,0:T(8,128)(2,1)} %get-tuple-element.32), channel_id=1, replica_groups=mesh['op'=16,'sec'=8] {'op'}, dimensions={0} | all-to-all | bytes 33554432 | tf_op jit(solution)/shard_map/all_to_all | solution.py:46
  700.9 9.5 %fusion.12 = f32[2,256,4,256]{3,1,2,0:T(8,128)} fusion(bf16[2,16,1,256,256]{4,3,2,1,0:T(8,128)(2,1)S(1)} %copy-done.2, bf16[16,2,1,256,4,256]{5,3,4,2,1,0:T(8,128)(2,1)} %bitcast.48), kind=kOutput, calls=%fused_computation.16 | convolution fusion | flops 4294967296 | bytes 23068672 | tf_op jit(solution)/shard_map/sklqm,skrm->slqr/dot_general | solution.py:48
  710.5 70.5 %all-reduce.2.cloned.1.call-done = f32[2,256,4,256]{3,1,2,0:T(8,128)} async-done(((f32[2,256,4,256]{3,1,2,0:T(8,128)}), f32[2,256,4,256]{3,1,2,0:T(8,128)}) %all-reduce.2.cloned.1.call-update) | async-done | bytes 2097168 | tf_op jit(solution)/shard_map/psum | solution.py:52
  (120 shorter events, 128.1 us)
Async XLA Ops:
  6.5 17.6 %copy-start = (f32[128,4,4]{0,2,1:T(4,128)S(1)}, f32[128,4,4]{0,2,1:T(4,128)}, u32[]{:S(2)}) copy-start(f32[128,4,4]{0,2,1:T(4,128)} %param.11) | copy-start | bytes 24580
  16.9 300.3 %all-to-all-start = ((bf16[32,256,4,256]{3,2,1,0:T(4,128)(2,1)}), bf16[32,256,4,256]{3,2,1,0:T(4,128)(2,1)}, u32[]{:S(2)}, u32[]{:S(2)}) async-start(bf16[32,256,4,256]{3,2,1,0:T(4,128)(2,1)} %bitcast.47), calls=%async_computation | async-start | bytes 33554432 | tf_op jit(solution)/shard_map/all_to_all | solution.py:10
  24.1 757.0 %all-reduce.2.cloned.1.call-start = ((), (), s32[]{:S(2)}) async-start(), calls=%async_computation.2 | async-start | bytes 4194304 | tf_op jit(solution)/shard_map/psum | solution.py:52
  503.2 197.7 %copy-start.2 = (bf16[2,16,1,256,256]{4,3,2,1,0:T(8,128)(2,1)S(1)}, bf16[2,16,1,256,256]{4,3,2,1,0:T(8,128)(2,1)}, u32[]{:S(2)}) copy-start(bf16[2,16,1,256,256]{4,3,2,1,0:T(8,128)(2,1)} %param.10) | copy-start | bytes 12582916
  700.9 82.0 %copy-start.1 = (f32[128,4,4]{0,2,1:T(4,128)S(1)}, f32[128,4,4]{0,2,1:T(4,128)}, u32[]{:S(2)}) copy-start(f32[128,4,4]{0,2,1:T(4,128)} %param.11) | copy-start | bytes 24580
Sparse Core Ops, SparseCore 0:
  710.6 70.4 all-reduce.1
